TPU v7x, 256 devices: a whole 4x4x8 slice. The times are simulated.
256 devices in a mesh: tm: 8 (over z), lat: 4 (over x), lon: 8 (over y, core).
Axes of the slice: x: 4, y: 4, z: 8, core: 2. Of those that a mesh axis runs over, the one named last changes fastest.
Arguments:
- slab: bfloat16 [512, 262144], P('tm', ('lat', 'lon')), may hold values from -6 to 6
- start: bfloat16 [512, 64], P('tm'), may hold values from -6 to 6
- sections: float32 [3, 2], replicated, may hold values from 0.2 to 1.5708, as said below
Outputs:
- basis: float32 [2048, 64, 128], P(('lat', 'lon', 'tm'))
- pcs: float32 [512, 64], P('tm')
Inputs may be any that keep to these rules, and one draw needn't show every extreme that they name: `sections`: in each column, one section has radius 0.78 to 0.86 and angle 2 pi / 8 to 2 pi / 4, the other radius 0.9955 to 0.9985 and angle 2 pi / 24 to 2 pi / 12; which column is which varies; amplitudes 0.2 to 1.0.
All inputs are finite; a program needn't handle non-finite values.
Results may differ from a plain program's by a relative error of at most 0.0039.
Values may be sent and summed in bfloat16 or wider, within the bound.
A program may use at most 64 MiB of HBM per device.

v0:
```python
import math
import jax
import jax.numpy as jnp
from jax import lax
from jax.sharding import PartitionSpec as P

LANES = 128
TOP_PRECISION = lax.Precision.HIGHEST


def prefix(value, axis, join, neutral):
    count, mine = (lax.axis_size(axis), lax.axis_index(axis))
    pieces = jax.tree.map(lambda part: lax.all_gather(part, axis), value)
    running = jax.tree.map(
        lambda part, zero: jnp.full_like(part, 0) + jnp.asarray(zero, part.dtype), value, neutral
    )

    def step(position, running):
        longer = join(running, jax.tree.map(lambda part: part[position], pieces))
        return jax.tree.map(lambda new, old: jnp.where(position < mine, new, old), longer, running)

    return lax.fori_loop(0, count - 1, step, running)


def impulse(radius, angle, steps):
    counted = jnp.maximum(steps, 0).astype(jnp.float32)
    values = jnp.exp(counted * jnp.log(radius)) * jnp.sin((counted + 1.0) * angle) / jnp.sin(angle)
    return jnp.where(steps >= 0, values, 0.0)


def section_columns(radius, angle, feed_two, drive_gain, times):
    return [
        -drive_gain * impulse(radius, angle, times - 1),
        -drive_gain * impulse(radius, angle, times),
        impulse(radius, angle, times + 1),
        feed_two * impulse(radius, angle, times),
    ]


def block_maps(sections, hour_count):
    radius = sections[0]
    angles = sections[1]
    amplitude = sections[2]
    feed_two = -radius * radius
    drive_gain = amplitude * jnp.sqrt(1.0 - radius * radius)
    hours = jnp.arange(hour_count, dtype=jnp.int32)
    lag = hours[:, None] - hours[None, :]
    drive_rows = jnp.zeros((hour_count, hour_count), jnp.float32)
    input_rows = [
        (hours == hour_count - 1).astype(jnp.float32),
        (hours == hour_count - 2).astype(jnp.float32),
    ]
    state_parts = []
    end_rows = [jnp.zeros((6,), jnp.float32), jnp.zeros((6,), jnp.float32)]
    for section in range(2):
        rad = radius[section]
        ang = angles[section]
        drive_rows = drive_rows + drive_gain[section] * (
            impulse(rad, ang, lag) - impulse(rad, ang, lag - 2)
        )
        for back in range(2):
            ahead = hour_count - 1 - back - hours
            input_rows.append(
                drive_gain[section] * (impulse(rad, ang, ahead) - impulse(rad, ang, ahead - 2))
            )
        state_parts.append(section_columns(rad, ang, feed_two[section], drive_gain[section], hours))
        for back in range(2):
            moment = jnp.array(hour_count - 1 - back, jnp.int32)
            pieces = section_columns(rad, ang, feed_two[section], drive_gain[section], moment)
            zeros_pair = [jnp.zeros((), jnp.float32), jnp.zeros((), jnp.float32)]
            own = pieces[2:] + zeros_pair if section == 0 else zeros_pair + pieces[2:]
            end_rows.append(jnp.stack(pieces[:2] + own))
    first, second = state_parts
    state_rows = jnp.stack(
        [first[0] + second[0], first[1] + second[1], first[2], first[3], second[2], second[3]],
        axis=1,
    )
    end_inputs = jnp.stack(input_rows)
    end_state = jnp.stack(end_rows)
    return (drive_rows, end_inputs, state_rows, end_state)


def combine(earlier, subsequent):
    concatenated_rows = jnp.dot(subsequent[0], earlier[0], precision=TOP_PRECISION)
    vector = jnp.dot(subsequent[0], earlier[1], precision=TOP_PRECISION) + subsequent[1]
    return (concatenated_rows, vector)


def make_orthonormal(spatial_patterns):
    local_gram_block = jnp.einsum(
        "zrs,zts->rt", spatial_patterns, spatial_patterns, precision=TOP_PRECISION
    )
    gram_matrix = lax.psum(local_gram_block, ("tm", "lat", "lon"))
    lower_factor = jnp.linalg.cholesky(gram_matrix)
    width = gram_matrix.shape[0]
    inverse_factor = jax.scipy.linalg.solve_triangular(
        lower_factor, jnp.eye(width, dtype=jnp.float32), lower=True
    )
    return jnp.einsum("de,wes->wds", inverse_factor, spatial_patterns, precision=TOP_PRECISION)


def local(slab, start, sections):
    hour_count, cell_count = slab.shape
    width = start.shape[1]
    drive_rows, end_inputs, state_rows, end_state = block_maps(sections, hour_count)
    values = slab.astype(jnp.float32)
    local_part = jnp.dot(drive_rows, values, precision=TOP_PRECISION)
    leaving = jnp.dot(end_inputs, values, precision=TOP_PRECISION)
    identity_pair = (jnp.eye(6, dtype=jnp.float32), jnp.zeros_like(leaving))
    entering = prefix((end_state, leaving), "tm", combine, identity_pair)[1]
    filtered = (local_part + jnp.dot(state_rows, entering, precision=TOP_PRECISION)).astype(
        jnp.bfloat16
    )
    grouped = filtered.reshape(hour_count, cell_count // LANES, LANES)
    cells_all = cell_count * lax.axis_size("lat") * lax.axis_size("lon")
    hours_all = hour_count * lax.axis_size("tm")
    block_of_rows = grouped
    spatial_patterns = lax.psum_scatter(
        jnp.einsum("tk,tgc->gkc", start, block_of_rows, preferred_element_type=jnp.float32),
        "tm",
        scatter_dimension=0,
        tiled=True,
    )
    ortho = make_orthonormal(spatial_patterns)
    block_of_rows = grouped.astype(jnp.float32)
    partial_sums = jnp.zeros((hour_count, width), jnp.float32) + jnp.einsum(
        "tgc,gkc->tk",
        block_of_rows,
        lax.all_gather(ortho.astype(jnp.bfloat16), "tm", axis=0, tiled=True).astype(jnp.float32),
        precision=TOP_PRECISION,
    )
    projections = lax.psum(partial_sums, ("lat", "lon"))
    basis = ortho * math.sqrt(cells_all)
    pcs = projections * math.sqrt(hours_all / cells_all)
    return (basis, pcs)


def solution(mesh):
    return jax.shard_map(
        local,
        mesh=mesh,
        in_specs=(P("tm", ("lat", "lon")), P("tm", None), P()),
        out_specs=(P(("lat", "lon", "tm"), None, None), P("tm", None)),
        check_vma=False,
    )
```

profile of v0, /device:TPU:32, one launch (start us, length us, event | category | flops | bytes accessed | tf_op | source)
XLA Modules:
  0.0 378.2 jit_solution(5782166197295645485)
XLA Ops:
  7.2 0.0 copy-start
  7.2 0.0 all-gather.9.cloned.1.call-start
  7.2 1.0 slice_reduce_fusion
  8.2 1.5 fusion.87
  9.7 0.7 fusion.89
  13.1 1.4 fusion.80
  14.5 1.4 fusion.79
  15.9 0.0 copy-done
  15.9 1.2 convolution_bitcast_fusion
  17.2 0.0 all-gather.9.cloned.1.call-update
  17.2 0.0 reduce-scatter.2.cloned.1.call-start
  20.7 0.7 fusion.88
  28.1 0.1 stack.99
  28.2 0.1 stack.94
  28.2 0.1 stack.110
  28.3 0.1 stack.105
  28.4 1.3 compare_select_fusion.9
  29.7 1.9 multiply_add_fusion.1
  31.7 1.3 compare_select_fusion.8
  33.0 27.4 %all-gather.2 = f32[8,6,6]{2,1,0:T(8,128)S(1)} all-gather(f32[1,6,6]{2,1,0:T(8,128)S(1)} %bitcast.79), channel_id=2, replica_groups=mesh['tm'=8,'lat'=4,'lon'=8] {'tm'}, dimensions={0}, use_global_device_ids=true | all-gather | bytes 1296 | tf_op jit(solution)/shard_map/all_gather | solution.py:13
  60.4 0.1 all-gather.9.cloned.1.call-done
  60.5 9.5 %while.14 = (s32[]{:T(128)}, f32[6,8192]{1,0:T(8,128)S(1)}, s32[]{:T(128)}, f32[8,6,6]{2,1,0:T(8,128)S(1)}, f32[8,6,8192]{2,1,0:T(8,128)}, /*index=5*/s32[]{:T(128)}, s32[]{:T(128)}) while((s32[]{:T(128)}, f32[6,8192]{1,0:T(8,128)S(1)}, s32[]{:T(128)}, f32[8,6,6]{2,1,0:T(8,128)S(1)}, f32[8,6,8192]{2,1,0:T(8,128)}, ...), condition=%wide.region_1.2_spmd.clone, body=%wide.region_0.1_spmd.clone.sunk | while | flops 3735556 | bytes 1317479 | solution.py:22
  60.5 1.3 fusion.106
  61.9 1.3 fusion.106
  63.3 1.3 fusion.106
  64.6 1.3 fusion.106
  66.0 1.3 fusion.106
  67.4 1.3 fusion.106
  68.7 1.3 fusion.106
  70.0 1.8 fusion.90
  71.9 0.0 copy-start.1
  71.9 4.2 %fusion.9 = bf16[8,64,8,128]{3,2,1,0:T(8,128)(2,1)S(1)} fusion(f32[64,8192]{1,0:T(8,128)S(1)} %fusion.90, bf16[64,8192]{1,0:T(8,128)(2,1)S(1)} %copy-done, f32[]{:T(128)S(6)} %sin.238, f32[]{:T(128)} %bitcast.5, f32[]{:T(128)} %bitcast.4, f32[]{:T(128)} %bitcast.3, f32[]{:T(128)S(6)} %sin.235, f32[]{:T(128)} %bitcast.2, f32[]{:T(128)} %bitcast.1, f32[]{:T(128)} %bitcast), kind=kOutput, calls=%fused_computation.13 | convolution fusion | flops 403845120 | bytes 4194336 | tf_op jit(solution)/shard_map/dot_general | solution.py:107
  76.1 0.0 copy-done.1
  76.1 1.8 convolution_bitcast_fusion.1
  77.9 0.0 reduce-scatter.2.cloned.1.call-update
  78.0 0.0 all-gather.7.cloned.1.call-start
  78.0 42.0 %reduce-scatter.2.cloned.1.call-done = f32[8,64,128]{2,1,0:T(8,128)} async-done(((f32[64,64,128]{2,1,0:T(8,128)}), f32[8,64,128]{2,1,0:T(8,128)}) %reduce-scatter.2.cloned.1.call-update) | async-done | bytes 262160 | tf_op jit(solution)/shard_map/reduce_scatter | solution.py:118
  120.0 1.4 convolution_bitcast_fusion.4
  121.4 74.9 %psum.14 = f32[64,64]{0,1:T(8,128)S(1)} all-reduce(f32[64,64]{0,1:T(8,128)S(1)} %convolution_bitcast_fusion.4), channel_id=1, replica_groups=mesh['tm'=8,'lat'=4,'lon'=8] {'tm','lat','lon'}, use_global_device_ids=true, to_apply=%region_3.4 | all-reduce | flops 4096 | bytes 32768 | tf_op jit(solution)/shard_map/psum | solution.py:93
  196.4 0.1 copy.13
  196.5 5.8 %cholesky.16 = f32[64,64]{1,0:T(8,128)S(1)} custom-call(f32[64,64]{1,0:T(8,128)S(1)} %fusion.16), custom_call_target="Cholesky" | custom-call | tf_op jit(solution)/shard_map/jit(cholesky)/cholesky | solution.py:94
  202.3 0.6 compare_reduce_fusion
  203.0 0.7 fusion.14
  203.6 4.9 %custom-call.7 = f32[1,64,64]{1,2,0:T(8,128)S(1)} custom-call(f32[1,64,64]{2,1,0:T(8,128)S(1)} %fusion.14), custom_call_target="InvertDiagBlocksLowerTriangular" | custom-call | tf_op jit(solution)/shard_map/jit(_solve_triangular)/triangular_solve | solution.py:96
  208.5 0.2 convolution_bitcast_fusion.3
  208.8 2.1 convert_bitcast_fusion
  210.8 0.0 all-gather.7.cloned.1.call-update
  210.9 34.8 %all-gather.7.cloned.1.call-done = bf16[64,64,128]{2,1,0:T(8,128)(2,1)} async-done(((bf16[8,64,128]{2,1,0:T(8,128)(2,1)}), bf16[64,64,128]{2,1,0:T(8,128)(2,1)}) %all-gather.7.cloned.1.call-update) | async-done | bytes 1048592 | tf_op jit(solution)/shard_map/all_gather | solution.py:129
  245.6 1.6 convolution_bitcast_fusion.2
  247.3 123.8 %psum.15 = f32[64,64]{1,0:T(8,128)S(1)} all-reduce(f32[64,64]{1,0:T(8,128)S(1)} %convolution_bitcast_fusion.2), channel_id=1, replica_groups=mesh['tm'=8,'lat'=4,'lon'=8] {'lat','lon'}, use_global_device_ids=true, to_apply=%region_6.7 | all-reduce | flops 4096 | bytes 32768 | tf_op jit(solution)/shard_map/psum | solution.py:132
  371.1 0.6 broadcast_multiply_fusion
  (17 shorter events, 0.3 us)
Async XLA Ops:
  7.2 8.8 %copy-start = (bf16[64,8192]{1,0:T(8,128)(2,1)S(1)}, bf16[64,8192]{1,0:T(8,128)(2,1)}, u32[]{:S(2)}) copy-start(bf16[64,8192]{1,0:T(8,128)(2,1)} %param.5) | copy-start | bytes 3145732
  7.2 53.3 %all-gather.9.cloned.1.call-start = ((), (), s32[]{:S(2)}) async-start(), calls=%async_computation.3 | async-start | bytes 2359296 | tf_op jit(solution)/shard_map/all_gather | solution.py:13
  17.2 102.8 %reduce-scatter.2.cloned.1.call-start = ((), (), s32[]{:S(2)}) async-start(), calls=%async_computation.1 | async-start | bytes 2359296 | tf_op jit(solution)/shard_map/reduce_scatter | solution.py:118
  71.9 4.2 %copy-start.1 = (bf16[64,64]{1,0:T(8,128)(2,1)S(1)}, bf16[64,64]{1,0:T(8,128)(2,1)}, u32[]{:S(2)}) copy-start(bf16[64,64]{1,0:T(8,128)(2,1)} %param.6) | copy-start | bytes 24580
  78.0 167.7 %all-gather.7.cloned.1.call-start = ((), (), s32[]{:S(2)}) async-start(), calls=%async_computation.2 | async-start | bytes 1179648 | tf_op jit(solution)/shard_map/all_gather | solution.py:129
Sparse Core Ops, SparseCore 0:
  17.3 43.1 all-gather.8
  78.1 41.8 reduce-scatter.1
  211.0 34.6 all-gather.6
where the time goes:
time: 379 us; the launch traced here: 378 us
  blocking collectives  226 us (60%)
  waiting for transfers between devices  76.9 us (20%)
  between operations  26.8 us (7%)
  matrix products  23.6 us (6%)
  other arithmetic  20 us (5%)
  local copies, waits for them, and re-layouts  4.4 us (1%)
    psum x1, blocking collectives, local(): projections = lax.psum(partial_sums, ('lat', 'lon'))  124 us
    psum x1, blocking collectives, make_orthonormal(): gram_matrix = lax.psum(local_gram_block, ('tm', 'lat', 'lon'))  74.9 us
    reduce_scatter x1, waiting for transfers between devices, local(): lax.psum_scatter(jnp.einsum('tk,tgc->gkc', start, block_of_rows, preferre...  42 us
    all_gather x1, waiting for transfers between devices, local(): lax.all_gather(ortho.astype(jnp.bfloat16), 'tm', axis=0, tiled=True)  34.8 us
    all_gather x1, blocking collectives, prefix(): pieces = jax.tree.map(lambda part: lax.all_gather(part, axis), value)  27.4 us
    dot_general x7, matrix products, combine(): jnp.dot(subsequent[0], earlier[1], precision=TOP_PRECISION) + subsequent[1]  9.15 us
  transfers between devices with their start and end apart: 3, of which 3 were waited for; matrix products, arithmetic and copies ran while one was open for 1% of the time, Pallas kernels for 0%

commit v1 on v0

--- a/solution.py
+++ b/solution.py
@@ -90,7 +90,7 @@
     local_gram_block = jnp.einsum(
         "zrs,zts->rt", spatial_patterns, spatial_patterns, precision=TOP_PRECISION
     )
-    gram_matrix = lax.psum(local_gram_block, ("tm", "lat", "lon"))
+    gram_matrix = jnp.sum(lax.all_gather(local_gram_block, ("tm", "lat", "lon")), axis=0)
     lower_factor = jnp.linalg.cholesky(gram_matrix)
     width = gram_matrix.shape[0]
     inverse_factor = jax.scipy.linalg.solve_triangular(

time: 379 us -> 428 us (1.13)
  waiting for transfers between devices: 76.9 us -> 196 us
  blocking collectives: 226 us -> 151 us
  other arithmetic: 20 us -> 24.3 us
    all_gather x0 -> x1, waiting for transfers between devices: none -> 119 us  [make_orthonormal(): lax.all_gather(local_gram_block, ('tm', 'lat', 'lon'))]
    psum x1 -> x0, blocking collectives: 74.9 us -> none  [make_orthonormal(): gram_matrix = lax.psum(local_gram_block, ('tm', 'lat', 'lon'))]
  transfers between devices with their start and end apart: 3 -> 4, of which waited for: 3 -> 3; matrix products, arithmetic and copies ran while one was open for 1% -> 1% of each run, Pallas kernels for 0% -> 0%
where the time goes in v1:
time: 428 us; the launch traced here: 427 us
  waiting for transfers between devices  196 us (46%)
  blocking collectives  151 us (35%)
  between operations  27 us (6%)
  other arithmetic  24.3 us (6%)
  matrix products  23.3 us (5%)
  local copies, waits for them, and re-layouts  4.33 us (1%)
    psum x1, blocking collectives, local(): projections = lax.psum(partial_sums, ('lat', 'lon'))  124 us
    all_gather x1, waiting for transfers between devices, make_orthonormal(): lax.all_gather(local_gram_block, ('tm', 'lat', 'lon'))  119 us
    reduce_scatter x1, waiting for transfers between devices, local(): lax.psum_scatter(jnp.einsum('tk,tgc->gkc', start, block_of_rows, preferre...  42 us
    all_gather x1, waiting for transfers between devices, local(): lax.all_gather(ortho.astype(jnp.bfloat16), 'tm', axis=0, tiled=True)  35.6 us
    all_gather x1, blocking collectives, prefix(): pieces = jax.tree.map(lambda part: lax.all_gather(part, axis), value)  27.5 us
    dot_general x7, matrix products, combine(): jnp.dot(subsequent[0], earlier[1], precision=TOP_PRECISION) + subsequent[1]  9.15 us
  transfers between devices with their start and end apart: 4, of which 3 were waited for; matrix products, arithmetic and copies ran while one was open for 1% of the time, Pallas kernels for 0%

profile of v1, /device:TPU:32, one launch (start us, length us, event | category | flops | bytes accessed | tf_op | source)
XLA Modules:
  0.0 426.8 jit_solution(18205603155161820418)
XLA Ops:
  7.2 0.0 copy-start
  7.2 0.0 all-gather.13.cloned.1.call-start
  7.2 1.0 slice_reduce_fusion
  8.2 1.5 fusion.87
  9.7 0.7 fusion.89
  13.2 1.4 fusion.80
  14.7 1.4 fusion.79
  16.1 0.0 copy-done
  16.1 1.2 convolution_bitcast_fusion
  17.3 0.0 all-gather.13.cloned.1.call-update
  17.3 0.0 reduce-scatter.2.cloned.1.call-start
  20.9 0.6 fusion.88
  28.2 0.1 stack.99
  28.3 0.1 stack.94
  28.4 0.1 stack.110
  28.5 0.1 stack.105
  28.6 1.4 compare_select_fusion.9
  30.0 1.9 multiply_add_fusion.1
  31.9 1.4 compare_select_fusion.8
  33.3 27.5 %all-gather.3 = f32[8,6,6]{2,1,0:T(8,128)S(1)} all-gather(f32[1,6,6]{2,1,0:T(8,128)S(1)} %bitcast.81), channel_id=2, replica_groups=mesh['tm'=8,'lat'=4,'lon'=8] {'tm'}, dimensions={0}, use_global_device_ids=true | all-gather | bytes 1296 | tf_op jit(solution)/shard_map/all_gather | solution.py:13
  60.8 0.0 all-gather.13.cloned.1.call-done
  60.8 9.5 %while.14 = (s32[]{:T(128)}, f32[6,8192]{1,0:T(8,128)S(1)}, s32[]{:T(128)}, f32[8,6,6]{2,1,0:T(8,128)S(1)}, f32[8,6,8192]{2,1,0:T(8,128)}, /*index=5*/s32[]{:T(128)}, s32[]{:T(128)}) while((s32[]{:T(128)}, f32[6,8192]{1,0:T(8,128)S(1)}, s32[]{:T(128)}, f32[8,6,6]{2,1,0:T(8,128)S(1)}, f32[8,6,8192]{2,1,0:T(8,128)}, ...), condition=%wide.region_1.2_spmd.clone, body=%wide.region_0.1_spmd.clone.sunk | while | flops 3735556 | bytes 1317479 | solution.py:22
  60.8 1.3 fusion.106
  62.2 1.3 fusion.106
  63.5 1.3 fusion.106
  64.9 1.3 fusion.106
  66.3 1.3 fusion.106
  67.6 1.3 fusion.106
  69.0 1.3 fusion.106
  70.3 1.8 fusion.90
  72.2 0.0 copy-start.2
  72.2 4.3 fusion.9
  76.5 0.0 copy-done.2
  76.5 1.8 convolution_bitcast_fusion.1
  78.3 0.0 reduce-scatter.2.cloned.1.call-update
  78.3 0.0 all-gather.11.cloned.1.call-start
  78.4 42.0 %reduce-scatter.2.cloned.1.call-done = f32[8,64,128]{2,1,0:T(8,128)} async-done(((f32[64,64,128]{2,1,0:T(8,128)}), f32[8,64,128]{2,1,0:T(8,128)}) %reduce-scatter.2.cloned.1.call-update) | async-done | bytes 262160 | tf_op jit(solution)/shard_map/reduce_scatter | solution.py:118
  120.4 2.0 convolution_bitcast_fusion.4
  122.4 0.0 all-gather.11.cloned.1.call-update
  122.4 0.0 all-gather.9.cloned.1.call-start
  122.5 118.6 %all-gather.11.cloned.1.call-done = f32[16384,64]{1,0:T(8,128)} async-done(((f32[64,64]{1,0:T(8,128)}), f32[16384,64]{1,0:T(8,128)}) %all-gather.11.cloned.1.call-update) | async-done | bytes 4194320 | tf_op jit(solution)/shard_map/all_gather | solution.py:93
  241.0 0.0 copy-start.1
  241.0 4.1 reduce_sum.9
  245.1 0.1 copy.11
  245.2 5.8 %cholesky.16 = f32[64,64]{1,0:T(8,128)S(1)} custom-call(f32[64,64]{1,0:T(8,128)S(1)} %fusion.16), custom_call_target="Cholesky" | custom-call | tf_op jit(solution)/shard_map/jit(cholesky)/cholesky | solution.py:94
  251.1 0.6 compare_reduce_fusion
  251.7 0.7 fusion.14
  252.4 4.9 %custom-call.7 = f32[1,64,64]{1,2,0:T(8,128)S(1)} custom-call(f32[1,64,64]{2,1,0:T(8,128)S(1)} %fusion.14), custom_call_target="InvertDiagBlocksLowerTriangular" | custom-call | tf_op jit(solution)/shard_map/jit(_solve_triangular)/triangular_solve | solution.py:96
  257.3 0.2 convolution_bitcast_fusion.3
  257.5 0.0 copy-done.1
  257.5 1.1 convert_bitcast_fusion
  258.6 0.0 all-gather.9.cloned.1.call-update
  258.7 35.6 %all-gather.9.cloned.1.call-done = bf16[64,64,128]{2,1,0:T(8,128)(2,1)} async-done(((bf16[8,64,128]{2,1,0:T(8,128)(2,1)}), bf16[64,64,128]{2,1,0:T(8,128)(2,1)}) %all-gather.9.cloned.1.call-update) | async-done | bytes 1048592 | tf_op jit(solution)/shard_map/all_gather | solution.py:129
  294.3 1.6 convolution_bitcast_fusion.2
  295.9 123.8 %psum.7 = f32[64,64]{1,0:T(8,128)S(1)} all-reduce(f32[64,64]{1,0:T(8,128)S(1)} %convolution_bitcast_fusion.2), channel_id=1, replica_groups=mesh['tm'=8,'lat'=4,'lon'=8] {'lat','lon'}, use_global_device_ids=true, to_apply=%region_6.7 | all-reduce | flops 4096 | bytes 32768 | tf_op jit(solution)/shard_map/psum | solution.py:132
  419.7 0.6 broadcast_multiply_fusion
  (17 shorter events, 0.3 us)
Async XLA Ops:
  7.2 8.9 %copy-start = (bf16[64,8192]{1,0:T(8,128)(2,1)S(1)}, bf16[64,8192]{1,0:T(8,128)(2,1)}, u32[]{:S(2)}) copy-start(bf16[64,8192]{1,0:T(8,128)(2,1)} %param.5) | copy-start | bytes 3145732
  7.2 53.6 %all-gather.13.cloned.1.call-start = ((), (), s32[]{:S(2)}) async-start(), calls=%async_computation.4 | async-start | bytes 2359296 | tf_op jit(solution)/shard_map/all_gather | solution.py:13
  17.3 103.1 %reduce-scatter.2.cloned.1.call-start = ((), (), s32[]{:S(2)}) async-start(), calls=%async_computation.1 | async-start | bytes 2359296 | tf_op jit(solution)/shard_map/reduce_scatter | solution.py:118
  72.2 4.3 %copy-start.2 = (bf16[64,64]{1,0:T(8,128)(2,1)S(1)}, bf16[64,64]{1,0:T(8,128)(2,1)}, u32[]{:S(2)}) copy-start(bf16[64,64]{1,0:T(8,128)(2,1)} %param.6) | copy-start | bytes 24580
  78.3 162.7 %all-gather.11.cloned.1.call-start = ((), (), s32[]{:S(2)}) async-start(), calls=%async_computation.3 | async-start | bytes 8421376 | tf_op jit(solution)/shard_map/all_gather | solution.py:93
  122.4 171.8 %all-gather.9.cloned.1.call-start = ((), (), s32[]{:S(2)}) async-start(), calls=%async_computation.2 | async-start | bytes 1179648 | tf_op jit(solution)/shard_map/all_gather | solution.py:129
  241.0 16.5 %copy-start.1 = (f32[8,64,128]{2,1,0:T(8,128)S(1)}, f32[8,64,128]{2,1,0:T(8,128)}, u32[]{:S(2)}) copy-start(f32[8,64,128]{2,1,0:T(8,128)} %reduce-scatter.2.cloned.1.call-done) | copy-start | bytes 786436
Sparse Core Ops, SparseCore 0:
  17.5 42.9 all-gather.12
  78.5 41.8 reduce-scatter.1
  124.7 116.2 all-gather.10
  258.8 35.4 all-gather.8
